TPU v7x, 32 devices: a whole 2x2x4 slice. The times are simulated.
32 devices in a mesh: segment: 4 (over y, x), expert: 8 (over z, core).
Axes of the slice: x: 2, y: 2, z: 4, core: 2. Of those that a mesh axis runs over, the one named last changes fastest.
Arguments:
- state_up: bfloat16 [4, 64, 3584], P('segment', 'expert'), may hold values from -6 to 6
- state_down: bfloat16 [4, 64, 3584], P('segment', 'expert'), may hold values from -6 to 6
- feed_up: bfloat16 [1, 64, 3584], P(None, 'expert'), may hold values from -6 to 6
- feed_down: bfloat16 [1, 64, 3584], P(None, 'expert'), may hold values from -6 to 6
- routes: int32 [2, 2, 4, 64, 2], P(None, None, 'segment', 'expert'), may hold values from 0 to 7, all different within a row; in each aligned block of 8 rows (0 to 7, 8 to 15, ..., all dimensions but the last counted through in order) at most 2 rows name the same one
- mixing: float32 [2, 2, 4, 64, 2], P(None, None, 'segment', 'expert'), may hold values from 0.2 to 1
- norm_gain: float32 [4, 3584], P('segment'), may hold values from 0.5 to 1.5
- gate_weight: bfloat16 [4, 3584, 8192], P('segment', None, 'expert'), may hold values from -0.09375 to 0.09375
- up_weight: bfloat16 [4, 3584, 8192], P('segment', None, 'expert'), may hold values from -0.09375 to 0.09375
- down_weight: bfloat16 [4, 8192, 3584], P('segment', 'expert'), may hold values from -0.1875 to 0.1875
Outputs:
- final_up: bfloat16 [4, 64, 3584], P('segment', 'expert')
- final_down: bfloat16 [4, 64, 3584], P('segment', 'expert')
Inputs may be any that keep to these rules, and one draw needn't show every extreme that they name: `routes`: the 2 experts of a token differ. Within the rows of one device for one step, direction and section, at most 2 name any one expert, a bound that some block reaches.
All inputs are finite; a program needn't handle non-finite values.
Results may differ from a plain program's by a relative error of at most 0.0065.
Values may be sent and summed in bfloat16 or wider, within the bound.
A program may use at most 64 MiB of HBM per device.

v0:
```python
import jax
import jax.numpy as jnp
from jax import lax
from jax.sharding import PartitionSpec as P

EXPERTS = 8
TOP = 2
TICKS = 2
CAP = 2


norm_eps = 1e-06


def passed_along(block, axis, distance):
    devices = range(lax.axis_size(axis))
    route = [(i - distance, i) for i in devices if i - distance in devices]
    return lax.ppermute(block, axis, route)


def normed(state, gain_row):
    values = state.astype(jnp.float32)
    inv_scale = lax.rsqrt(jnp.mean(values * values, axis=-1, keepdims=True) + norm_eps)
    return (values * inv_scale * gain_row[None, :]).astype(jnp.bfloat16)


def pack_rows(normed_rows, route_rows, shards):
    count = route_rows.shape[0]
    width = normed_rows.shape[1]
    flat_expert = route_rows.reshape(-1)
    onehot = (flat_expert[:, None] == jnp.arange(EXPERTS, dtype=jnp.int32)[None, :]).astype(
        jnp.int32
    )
    slots = jnp.sum(jnp.cumsum(onehot, axis=0) * onehot, axis=1) - 1
    place = flat_expert * CAP + slots
    target = jnp.arange(EXPERTS * CAP, dtype=jnp.int32)
    select = jnp.any(target[:, None, None] == place.reshape(count, TOP)[None, :, :], axis=2).astype(
        jnp.bfloat16
    )
    packed = jnp.dot(select, normed_rows, preferred_element_type=jnp.float32).astype(jnp.bfloat16)
    spread = jnp.broadcast_to(packed.reshape(EXPERTS, 1, CAP, width), (EXPERTS, shards, CAP, width))
    return (spread.reshape(EXPERTS * shards, CAP, width), place)


def expert_rows(received, gate_dev, up_dev, down_dev):
    sources, count, width = received.shape
    flat_rows = received.reshape(sources * count, width)
    gate_val = jnp.dot(flat_rows, gate_dev, preferred_element_type=jnp.float32)
    up_val = jnp.dot(flat_rows, up_dev, preferred_element_type=jnp.float32)
    hidden = (jax.nn.silu(gate_val) * up_val).astype(jnp.bfloat16)
    piece = jnp.dot(hidden, down_dev, preferred_element_type=jnp.float32).astype(jnp.bfloat16)
    return piece.reshape(sources, count, width)


def unpack_rows(returned, place, weight_rows, state, shards):
    count = state.shape[0]
    width = state.shape[1]
    summed = jnp.sum(returned.reshape(EXPERTS, shards, CAP, width).astype(jnp.float32), axis=1)
    picked = jnp.take(summed.reshape(EXPERTS * CAP, width), place, axis=0).reshape(
        count, TOP, width
    )
    mixed = jnp.sum(picked * weight_rows[:, :, None], axis=1)
    return (state.astype(jnp.float32) + mixed).astype(jnp.bfloat16)


def body(
    state_up,
    state_down,
    feed_up,
    feed_down,
    routes,
    mixing,
    norm_gain,
    gate_weight,
    up_weight,
    down_weight,
):
    segment_index = lax.axis_index("segment")
    last_segment = lax.axis_size("segment") - 1
    shards = lax.axis_size("expert") // EXPERTS
    gate_dev = gate_weight[0]
    up_dev = up_weight[0]
    down_dev = down_weight[0]
    gain_row = norm_gain[0]
    upper = state_up[0]
    lower = state_down[0]
    for tick_index in range(TICKS):
        packed_up, place_up = pack_rows(normed(upper, gain_row), routes[tick_index, 0, 0], shards)
        packed_down, place_down = pack_rows(
            normed(lower, gain_row), routes[tick_index, 1, 0], shards
        )
        back_up = lax.all_to_all(
            expert_rows(
                lax.all_to_all(packed_up, "expert", split_axis=0, concat_axis=0, tiled=True),
                gate_dev,
                up_dev,
                down_dev,
            ),
            "expert",
            split_axis=0,
            concat_axis=0,
            tiled=True,
        )
        back_down = lax.all_to_all(
            expert_rows(
                lax.all_to_all(packed_down, "expert", split_axis=0, concat_axis=0, tiled=True),
                gate_dev,
                up_dev,
                down_dev,
            ),
            "expert",
            split_axis=0,
            concat_axis=0,
            tiled=True,
        )
        result_up = unpack_rows(back_up, place_up, mixing[tick_index, 0, 0], upper, shards)
        result_down = unpack_rows(back_down, place_down, mixing[tick_index, 1, 0], lower, shards)
        if tick_index + 1 < TICKS:
            moved_up = passed_along(result_up, "segment", 1)
            moved_down = passed_along(result_down, "segment", -1)
            upper = jnp.where(segment_index == 0, feed_up[tick_index], moved_up)
            lower = jnp.where(segment_index == last_segment, feed_down[tick_index], moved_down)
        else:
            upper = result_up
            lower = result_down
    return (upper[None], lower[None])


def solution(mesh):
    placed = (
        P("segment", "expert", None),
        P("segment", "expert", None),
        P(None, "expert", None),
        P(None, "expert", None),
        P(None, None, "segment", "expert", None),
        P(None, None, "segment", "expert", None),
        P("segment", None),
        P("segment", None, "expert"),
        P("segment", None, "expert"),
        P("segment", "expert", None),
    )
    return jax.shard_map(
        body,
        mesh=mesh,
        in_specs=placed,
        out_specs=(P("segment", "expert", None), P("segment", "expert", None)),
        check_vma=False,
    )
```

profile of v0, /device:TPU:0, one launch (start us, length us, event | category | flops | bytes accessed | tf_op | source)
XLA Modules:
  0.0 127.1 jit_solution(11465836169422850239)
XLA Ops:
  0.6 0.7 fusion.136
  3.9 1.0 fusion.80
  4.9 0.7 bitcast_add_fusion.1
  5.7 0.8 reduce
  6.5 1.1 convolution_convert_fusion.1
  7.5 0.7 reshape_reshape.14
  8.2 6.4 %all-to-all-start.4 = ((bf16[8,2,3584]{2,1,0:T(2,128)(2,1)}), bf16[8,2,3584]{2,1,0:T(2,128)(2,1)S(1)}, u32[]{:S(2)}, u32[]{:S(2)}) async-start(bf16[8,2,3584]{2,1,0:T(2,128)(2,1)} %reshape_reshape.14), calls=%async_computation.4 | async-start | bytes 229376 | tf_op jit(solution)/shard_map/all_to_all | solution.py:106
  14.7 0.7 slice_bitcast_fusion
  15.6 1.0 fusion.76
  16.6 1.1 convolution_convert_fusion.3
  17.7 0.7 reshape_reshape.12
  18.6 2.5 %all-to-all-done.4 = bf16[8,2,3584]{2,1,0:T(2,128)(2,1)S(1)} async-done(((bf16[8,2,3584]{2,1,0:T(2,128)(2,1)}), bf16[8,2,3584]{2,1,0:T(2,128)(2,1)S(1)}, u32[]{:S(2)}, u32[]{:S(2)}) %all-to-all-start.4) | async-done | bytes 114720 | tf_op jit(solution)/shard_map/all_to_all | solution.py:106
  21.1 3.4 %all-to-all-start = ((bf16[8,2,3584]{2,1,0:T(2,128)(2,1)}), bf16[8,2,3584]{2,1,0:T(2,128)(2,1)S(1)}, u32[]{:S(2)}, u32[]{:S(2)}) async-start(bf16[8,2,3584]{2,1,0:T(2,128)(2,1)} %reshape_reshape.12), calls=%async_computation | async-start | bytes 229376 | tf_op jit(solution)/shard_map/all_to_all | solution.py:94
  24.5 4.1 %fusion.18 = f32[16,1024]{1,0:T(8,128)S(1)} fusion(bf16[16,3584]{1,0:T(8,128)(2,1)S(1)} %reshape.203, bf16[1,3584,1024]{2,1,0:T(8,128)(2,1)} %param.19), kind=kOutput, calls=%fused_computation.22 | convolution fusion | flops 117440512 | bytes 7520256 | tf_op jit(solution)/shard_map/dot_general | solution.py:48
  28.7 7.2 %fusion.30 = bf16[16,3584]{1,0:T(8,128)(2,1)S(1)} fusion(bf16[1,1024,3584]{2,1,0:T(8,128)(2,1)} %param.21, bf16[16,3584]{1,0:T(8,128)(2,1)S(1)} %reshape.203, bf16[1,3584,1024]{2,1,0:T(8,128)(2,1)} %param.20, f32[16,1024]{1,0:T(8,128)S(1)} %fusion.18), kind=kOutput, calls=%fused_computation.30 | convolution fusion | flops 235036672 | bytes 14974976 | tf_op jit(solution)/shard_map/dot_general | solution.py:51
  35.9 0.7 reshape.204
  36.6 5.0 %all-to-all-start.5 = ((bf16[8,2,3584]{2,1,0:T(2,128)(2,1)}), bf16[8,2,3584]{2,1,0:T(2,128)(2,1)S(1)}, u32[]{:S(2)}, u32[]{:S(2)}) async-start(bf16[8,2,3584]{2,1,0:T(2,128)(2,1)} %reshape.204), calls=%async_computation.5 | async-start | bytes 229376 | tf_op jit(solution)/shard_map/all_to_all | solution.py:104
  41.7 4.1 %fusion.22 = f32[16,1024]{1,0:T(8,128)S(1)} fusion(bf16[16,3584]{1,0:T(8,128)(2,1)S(1)} %reshape.193, bf16[1,3584,1024]{2,1,0:T(8,128)(2,1)} %param.19), kind=kOutput, calls=%fused_computation.26 | convolution fusion | flops 117440512 | bytes 7520256 | tf_op jit(solution)/shard_map/dot_general | solution.py:48
  45.8 7.2 %fusion.24 = bf16[16,3584]{1,0:T(8,128)(2,1)S(1)} fusion(bf16[1,1024,3584]{2,1,0:T(8,128)(2,1)} %param.21, bf16[16,3584]{1,0:T(8,128)(2,1)S(1)} %reshape.193, bf16[1,3584,1024]{2,1,0:T(8,128)(2,1)} %param.20, f32[16,1024]{1,0:T(8,128)S(1)} %fusion.22), kind=kOutput, calls=%fused_computation.28 | convolution fusion | flops 235036672 | bytes 14974976 | tf_op jit(solution)/shard_map/dot_general | solution.py:51
  53.0 0.7 reshape.194
  53.7 5.1 %all-to-all-start.1 = ((bf16[8,2,3584]{2,1,0:T(2,128)(2,1)}), bf16[8,2,3584]{2,1,0:T(2,128)(2,1)S(1)}, u32[]{:S(2)}, u32[]{:S(2)}) async-start(bf16[8,2,3584]{2,1,0:T(2,128)(2,1)} %reshape.194), calls=%async_computation.1 | async-start | bytes 229376 | tf_op jit(solution)/shard_map/all_to_all | solution.py:92
  58.9 0.6 gather_fusion.2
  59.7 0.4 multiply_reduce_fusion.1
  60.1 1.3 %collective-permute-start.1 = (bf16[8,3584]{1,0:T(8,128)(2,1)S(1)}, bf16[8,3584]{1,0:T(8,128)(2,1)S(1)}, u32[]{:S(2)}, u32[]{:S(2)}) collective-permute-start(bf16[8,3584]{1,0:T(8,128)(2,1)S(1)} %fusion.83), channel_id=1, source_target_pairs={{8,0},{16,8},{24,16},{9,1},{17,9},{25,17},{10,2},{18,10},{26,18},{... | collective-permute-start | bytes 172040 | tf_op jit(solution)/shard_map/ppermute | solution.py:18
  61.4 3.9 %all-to-all-done.1 = bf16[8,2,3584]{2,1,0:T(2,128)(2,1)S(1)} async-done(((bf16[8,2,3584]{2,1,0:T(2,128)(2,1)}), bf16[8,2,3584]{2,1,0:T(2,128)(2,1)S(1)}, u32[]{:S(2)}, u32[]{:S(2)}) %all-to-all-start.1) | async-done | bytes 114720 | tf_op jit(solution)/shard_map/all_to_all | solution.py:92
  65.4 0.6 gather_fusion
  66.2 0.4 multiply_reduce_fusion.3
  66.6 3.4 %collective-permute-start = (bf16[8,3584]{1,0:T(8,128)(2,1)S(1)}, bf16[8,3584]{1,0:T(8,128)(2,1)S(1)}, u32[]{:S(2)}, u32[]{:S(2)}) collective-permute-start(bf16[8,3584]{1,0:T(8,128)(2,1)S(1)} %fusion.79), channel_id=1, source_target_pairs={{0,8},{8,16},{16,24},{1,9},{9,17},{17,25},{2,10},{10,18},{18,26},{... | collective-permute-start | bytes 172040 | tf_op jit(solution)/shard_map/ppermute | solution.py:18
  70.5 0.7 reshape_reshape.15
  71.2 3.4 %all-to-all-start.6 = ((bf16[8,2,3584]{2,1,0:T(2,128)(2,1)}), bf16[8,2,3584]{2,1,0:T(2,128)(2,1)S(1)}, u32[]{:S(2)}, u32[]{:S(2)}) async-start(bf16[8,2,3584]{2,1,0:T(2,128)(2,1)} %reshape_reshape.15), calls=%async_computation.6 | async-start | bytes 229376 | tf_op jit(solution)/shard_map/all_to_all | solution.py:106
  75.0 0.7 reshape_reshape.13
  75.6 5.4 %all-to-all-done.6 = bf16[8,2,3584]{2,1,0:T(2,128)(2,1)S(1)} async-done(((bf16[8,2,3584]{2,1,0:T(2,128)(2,1)}), bf16[8,2,3584]{2,1,0:T(2,128)(2,1)S(1)}, u32[]{:S(2)}, u32[]{:S(2)}) %all-to-all-start.6) | async-done | bytes 114720 | tf_op jit(solution)/shard_map/all_to_all | solution.py:106
  81.0 3.5 %all-to-all-start.2 = ((bf16[8,2,3584]{2,1,0:T(2,128)(2,1)}), bf16[8,2,3584]{2,1,0:T(2,128)(2,1)S(1)}, u32[]{:S(2)}, u32[]{:S(2)}) async-start(bf16[8,2,3584]{2,1,0:T(2,128)(2,1)} %reshape_reshape.13), calls=%async_computation.2 | async-start | bytes 229376 | tf_op jit(solution)/shard_map/all_to_all | solution.py:94
  84.6 4.1 %fusion.16 = f32[16,1024]{1,0:T(8,128)S(1)} fusion(bf16[16,3584]{1,0:T(8,128)(2,1)S(1)} %reshape.208, bf16[1,3584,1024]{2,1,0:T(8,128)(2,1)} %param.19), kind=kOutput, calls=%fused_computation.20 | convolution fusion | flops 117440512 | bytes 7520256 | tf_op jit(solution)/shard_map/dot_general | solution.py:48
  88.7 7.2 %fusion.33 = bf16[16,3584]{1,0:T(8,128)(2,1)S(1)} fusion(bf16[1,1024,3584]{2,1,0:T(8,128)(2,1)} %param.21, bf16[16,3584]{1,0:T(8,128)(2,1)S(1)} %reshape.208, bf16[1,3584,1024]{2,1,0:T(8,128)(2,1)} %param.20, f32[16,1024]{1,0:T(8,128)S(1)} %fusion.16), kind=kOutput, calls=%fused_computation.31 | convolution fusion | flops 235036672 | bytes 14974976 | tf_op jit(solution)/shard_map/dot_general | solution.py:51
  95.9 0.7 reshape.209
  96.6 4.8 %all-to-all-start.7 = ((bf16[8,2,3584]{2,1,0:T(2,128)(2,1)}), bf16[8,2,3584]{2,1,0:T(2,128)(2,1)S(1)}, u32[]{:S(2)}, u32[]{:S(2)}) async-start(bf16[8,2,3584]{2,1,0:T(2,128)(2,1)} %reshape.209), calls=%async_computation.7 | async-start | bytes 229376 | tf_op jit(solution)/shard_map/all_to_all | solution.py:104
  101.5 4.1 %fusion.20 = f32[16,1024]{1,0:T(8,128)S(1)} fusion(bf16[16,3584]{1,0:T(8,128)(2,1)S(1)} %reshape.198, bf16[1,3584,1024]{2,1,0:T(8,128)(2,1)} %param.19), kind=kOutput, calls=%fused_computation.24 | convolution fusion | flops 117440512 | bytes 7520256 | tf_op jit(solution)/shard_map/dot_general | solution.py:48
  105.7 7.2 %fusion.27 = bf16[16,3584]{1,0:T(8,128)(2,1)S(1)} fusion(bf16[1,1024,3584]{2,1,0:T(8,128)(2,1)} %param.21, bf16[16,3584]{1,0:T(8,128)(2,1)S(1)} %reshape.198, bf16[1,3584,1024]{2,1,0:T(8,128)(2,1)} %param.20, f32[16,1024]{1,0:T(8,128)S(1)} %fusion.20), kind=kOutput, calls=%fused_computation.29 | convolution fusion | flops 235036672 | bytes 14974976 | tf_op jit(solution)/shard_map/dot_general | solution.py:51
  112.9 0.7 reshape.199
  113.6 5.1 %all-to-all-start.3 = ((bf16[8,2,3584]{2,1,0:T(2,128)(2,1)}), bf16[8,2,3584]{2,1,0:T(2,128)(2,1)S(1)}, u32[]{:S(2)}, u32[]{:S(2)}) async-start(bf16[8,2,3584]{2,1,0:T(2,128)(2,1)} %reshape.199), calls=%async_computation.3 | async-start | bytes 229376 | tf_op jit(solution)/shard_map/all_to_all | solution.py:92
  118.7 0.6 gather_fusion.3
  119.6 0.4 multiply_reduce_fusion
  119.9 0.6 fusion.106
  120.6 4.6 %all-to-all-done.3 = bf16[8,2,3584]{2,1,0:T(2,128)(2,1)S(1)} async-done(((bf16[8,2,3584]{2,1,0:T(2,128)(2,1)}), bf16[8,2,3584]{2,1,0:T(2,128)(2,1)S(1)}, u32[]{:S(2)}, u32[]{:S(2)}) %all-to-all-start.3) | async-done | bytes 114720 | tf_op jit(solution)/shard_map/all_to_all | solution.py:92
  125.2 0.6 gather_fusion.1
  126.1 0.4 multiply_reduce_fusion.2
  126.5 0.6 fusion.108
  (87 shorter events, 5.2 us)
Async XLA Ops:
  8.2 12.9 %all-to-all-start.4 = ((bf16[8,2,3584]{2,1,0:T(2,128)(2,1)}), bf16[8,2,3584]{2,1,0:T(2,128)(2,1)S(1)}, u32[]{:S(2)}, u32[]{:S(2)}) async-start(bf16[8,2,3584]{2,1,0:T(2,128)(2,1)} %reshape_reshape.14), calls=%async_computation.4 | async-start | bytes 229376 | tf_op jit(solution)/shard_map/all_to_all | solution.py:106
  21.1 15.5 %all-to-all-start = ((bf16[8,2,3584]{2,1,0:T(2,128)(2,1)}), bf16[8,2,3584]{2,1,0:T(2,128)(2,1)S(1)}, u32[]{:S(2)}, u32[]{:S(2)}) async-start(bf16[8,2,3584]{2,1,0:T(2,128)(2,1)} %reshape_reshape.12), calls=%async_computation | async-start | bytes 229376 | tf_op jit(solution)/shard_map/all_to_all | solution.py:94
  36.6 17.1 %all-to-all-start.5 = ((bf16[8,2,3584]{2,1,0:T(2,128)(2,1)}), bf16[8,2,3584]{2,1,0:T(2,128)(2,1)S(1)}, u32[]{:S(2)}, u32[]{:S(2)}) async-start(bf16[8,2,3584]{2,1,0:T(2,128)(2,1)} %reshape.204), calls=%async_computation.5 | async-start | bytes 229376 | tf_op jit(solution)/shard_map/all_to_all | solution.py:104
  45.8 14.3 %copy-start = (bf16[1,8,3584]{2,1,0:T(8,128)(2,1)S(1)}, bf16[1,8,3584]{2,1,0:T(8,128)(2,1)}, u32[]{:S(2)}) copy-start(bf16[1,8,3584]{2,1,0:T(8,128)(2,1)} %param.13) | copy-start | bytes 172036
  53.0 13.6 %copy-start.1 = (bf16[1,8,3584]{2,1,0:T(8,128)(2,1)S(1)}, bf16[1,8,3584]{2,1,0:T(8,128)(2,1)}, u32[]{:S(2)}) copy-start(bf16[1,8,3584]{2,1,0:T(8,128)(2,1)} %param.12) | copy-start | bytes 172036
  53.0 17.0 %copy-start.2 = (bf16[1,8,3584]{2,1,0:T(8,128)(2,1)S(1)}, bf16[1,8,3584]{2,1,0:T(8,128)(2,1)}, u32[]{:S(2)}) copy-start(bf16[1,8,3584]{2,1,0:T(8,128)(2,1)} %param.15) | copy-start | bytes 172036
  53.0 21.5 %copy-start.3 = (bf16[1,8,3584]{2,1,0:T(8,128)(2,1)S(1)}, bf16[1,8,3584]{2,1,0:T(8,128)(2,1)}, u32[]{:S(2)}) copy-start(bf16[1,8,3584]{2,1,0:T(8,128)(2,1)} %param.14) | copy-start | bytes 172036
  53.7 11.6 %all-to-all-start.1 = ((bf16[8,2,3584]{2,1,0:T(2,128)(2,1)}), bf16[8,2,3584]{2,1,0:T(2,128)(2,1)S(1)}, u32[]{:S(2)}, u32[]{:S(2)}) async-start(bf16[8,2,3584]{2,1,0:T(2,128)(2,1)} %reshape.194), calls=%async_computation.1 | async-start | bytes 229376 | tf_op jit(solution)/shard_map/all_to_all | solution.py:92
  60.1 9.9 %collective-permute-start.1 = (bf16[8,3584]{1,0:T(8,128)(2,1)S(1)}, bf16[8,3584]{1,0:T(8,128)(2,1)S(1)}, u32[]{:S(2)}, u32[]{:S(2)}) collective-permute-start(bf16[8,3584]{1,0:T(8,128)(2,1)S(1)} %fusion.83), channel_id=1, source_target_pairs={{8,0},{16,8},{24,16},{9,1},{17,9},{25,17},{10,2},{18,10},{26,18},{... | collective-permute-start | bytes 172040 | tf_op jit(solution)/shard_map/ppermute | solution.py:18
  66.6 7.9 %collective-permute-start = (bf16[8,3584]{1,0:T(8,128)(2,1)S(1)}, bf16[8,3584]{1,0:T(8,128)(2,1)S(1)}, u32[]{:S(2)}, u32[]{:S(2)}) collective-permute-start(bf16[8,3584]{1,0:T(8,128)(2,1)S(1)} %fusion.79), channel_id=1, source_target_pairs={{0,8},{8,16},{16,24},{1,9},{9,17},{17,25},{2,10},{10,18},{18,26},{... | collective-permute-start | bytes 172040 | tf_op jit(solution)/shard_map/ppermute | solution.py:18
  71.2 9.8 %all-to-all-start.6 = ((bf16[8,2,3584]{2,1,0:T(2,128)(2,1)}), bf16[8,2,3584]{2,1,0:T(2,128)(2,1)S(1)}, u32[]{:S(2)}, u32[]{:S(2)}) async-start(bf16[8,2,3584]{2,1,0:T(2,128)(2,1)} %reshape_reshape.15), calls=%async_computation.6 | async-start | bytes 229376 | tf_op jit(solution)/shard_map/all_to_all | solution.py:106
  81.0 15.7 %all-to-all-start.2 = ((bf16[8,2,3584]{2,1,0:T(2,128)(2,1)}), bf16[8,2,3584]{2,1,0:T(2,128)(2,1)S(1)}, u32[]{:S(2)}, u32[]{:S(2)}) async-start(bf16[8,2,3584]{2,1,0:T(2,128)(2,1)} %reshape_reshape.13), calls=%async_computation.2 | async-start | bytes 229376 | tf_op jit(solution)/shard_map/all_to_all | solution.py:94
  96.6 16.9 %all-to-all-start.7 = ((bf16[8,2,3584]{2,1,0:T(2,128)(2,1)}), bf16[8,2,3584]{2,1,0:T(2,128)(2,1)S(1)}, u32[]{:S(2)}, u32[]{:S(2)}) async-start(bf16[8,2,3584]{2,1,0:T(2,128)(2,1)} %reshape.209), calls=%async_computation.7 | async-start | bytes 229376 | tf_op jit(solution)/shard_map/all_to_all | solution.py:104
  113.6 11.6 %all-to-all-start.3 = ((bf16[8,2,3584]{2,1,0:T(2,128)(2,1)}), bf16[8,2,3584]{2,1,0:T(2,128)(2,1)S(1)}, u32[]{:S(2)}, u32[]{:S(2)}) async-start(bf16[8,2,3584]{2,1,0:T(2,128)(2,1)} %reshape.199), calls=%async_computation.3 | async-start | bytes 229376 | tf_op jit(solution)/shard_map/all_to_all | solution.py:92
where the time goes:
time: 128 us; the launch traced here: 127 us
  matrix products  48 us (38%)
  starting transfers between devices  41.4 us (32%)
  waiting for transfers between devices  16.4 us (13%)
  local copies, waits for them, and re-layouts  12 us (9%)
  other arithmetic  8.32 us (6%)
    dot_general x4, matrix products, expert_rows(): jnp.dot(hidden, down_dev, preferred_element_type=jnp.float32)  28.8 us
    dot_general x4, matrix products, expert_rows(): gate_val = jnp.dot(flat_rows, gate_dev, preferred_element_type=jnp.float32)  16.6 us
    all_to_all x2, starting transfers between devices, body(): lax.all_to_all(expert_rows(lax.all_to_all(packed_up, 'expert', split_axis...  10.2 us
    all_to_all x2, starting transfers between devices, body(): lax.all_to_all(expert_rows(lax.all_to_all(packed_down, 'expert', split_ax...  9.87 us
    all_to_all x2, starting transfers between devices, body(): lax.all_to_all(packed_down, 'expert', split_axis=0, concat_axis=0, tiled=...  9.72 us
    all_to_all x2, waiting for transfers between devices, body(): lax.all_to_all(expert_rows(lax.all_to_all(packed_up, 'expert', split_axis...  8.57 us
    all_to_all x2, waiting for transfers between devices, body(): lax.all_to_all(packed_down, 'expert', split_axis=0, concat_axis=0, tiled=...  7.85 us
    all_to_all x2, starting transfers between devices, body(): lax.all_to_all(packed_up, 'expert', split_axis=0, concat_axis=0, tiled=True)  6.91 us
  transfers between devices with their start and end apart: 10, of which 4 were waited for; matrix products, arithmetic and copies ran while one was open for 46% of the time, Pallas kernels for 0%

commit v1 on v0

v1 whole, which is shorter than its diff:
```python
import functools

import jax
import jax.numpy as jnp
from jax import lax
from jax.experimental import pallas as pl
from jax.experimental.pallas import tpu as pltpu
from jax.sharding import PartitionSpec as P

EXPERTS = 8
TOP = 2
TICKS = 2
CAP = 2
DIRS = 2
LANES = 128
RPB = DIRS * CAP
QUADS = 16 // RPB
SPAN = QUADS * LANES
MESH = pl.DeviceIdType.MESH

norm_eps = 1e-06

RETURN_CUTS = (0, 2, 4, 7)
GATE_TILE = 256


def iota(shape, axis):
    return lax.broadcasted_iota(jnp.int32, shape, axis)


def stack(rows):
    chunks = rows.shape[1] // SPAN
    return jnp.concatenate(
        [
            jnp.concatenate(
                [rows[:, c * SPAN + q * LANES : c * SPAN + (q + 1) * LANES] for c in range(chunks)],
                axis=1,
            )
            for q in range(QUADS)
        ],
        axis=0,
    )


def unstack(rows, count):
    return jnp.concatenate(
        [
            rows[q * count : (q + 1) * count, c * LANES : (c + 1) * LANES]
            for c in range(rows.shape[1] // LANES)
            for q in range(QUADS)
        ],
        axis=1,
    )


def one_hot(condition):
    return jnp.where(condition, 1.0, 0.0).astype(jnp.bfloat16)


def select(matrix, rows):
    return jnp.dot(matrix, rows, preferred_element_type=jnp.float32)


def tables(routes, tokens):
    wide = DIRS * QUADS * tokens
    blocks = EXPERTS * 16
    eye = iota((tokens, LANES), 0) == iota((tokens, LANES), 1)
    before = iota((tokens, LANES), 1) < iota((tokens, LANES), 0)
    columns = [[] for _ in range(TOP)]
    for rows in routes:
        cols = [rows[:, k : k + 1] for k in range(TOP)]
        lying = [jnp.sum(jnp.where(eye, c, 0), axis=0, keepdims=True) for c in cols]
        for k in range(TOP):
            same = sum(jnp.where(before & (cols[k] == line), 1, 0) for line in lying)
            place = cols[k] * CAP + jnp.sum(same, axis=1, keepdims=True)
            columns[k] += [place] * QUADS
    columns = [jnp.concatenate(c, axis=0) for c in columns]
    big_eye = iota((wide, wide), 0) == iota((wide, wide), 1)
    i, j = iota((blocks, wide), 0), iota((blocks, wide), 1)
    slot = (i // 16) * CAP + i % CAP
    fits = ((i // CAP) % DIRS == j // (QUADS * tokens)) & (
        (i // RPB) % QUADS == (j // tokens) % QUADS
    )
    named = False
    for c in columns:
        named = named | (slot == jnp.sum(jnp.where(big_eye, c, 0), axis=0, keepdims=True))
    pack = one_hot(fits & named)
    i, j = iota((wide, blocks), 1), iota((wide, blocks), 0)
    slot = (i // 16) * CAP + i % CAP
    fits = ((i // CAP) % DIRS == j // (QUADS * tokens)) & (
        (i // RPB) % QUADS == (j // tokens) % QUADS
    )
    picks = [one_hot(fits & (slot == c)) for c in columns]
    return pack, jnp.concatenate(picks, axis=0)


def kernel(
    n,
    ns,
    up_ref,
    down_ref,
    feed_up_ref,
    feed_down_ref,
    routes_ref,
    mixing_ref,
    gain_ref,
    gate_hbm,
    upw_hbm,
    downw_hbm,
    out_up_ref,
    out_down_ref,
    gate_v,
    upw_v,
    downw_v,
    send_buf,
    recv_buf,
    back_buf,
    ret_buf,
    rows_buf,
    hidden_buf,
    move_src,
    move_dst,
    w_sem,
    d_send,
    d_recv,
    r_send,
    r_recv,
    m_send,
    m_recv,
):
    me = lax.axis_index("expert")
    seg = lax.axis_index("segment")
    shards = n // EXPERTS
    tokens = up_ref.shape[1]
    width = up_ref.shape[2]
    ff = gate_v.shape[1]
    tile = min(GATE_TILE, ff)
    cols = width // QUADS
    group_rows = EXPERTS * RPB

    w_copies = []
    for f in range(ff // tile):
        for hbm, vmem in ((gate_hbm, gate_v), (upw_hbm, upw_v)):
            at = pl.ds(f * tile, tile)
            w_copies.append(
                pltpu.make_async_copy(hbm.at[0, :, at], vmem.at[:, at], w_sem.at[len(w_copies)])
            )
    gate_copies = len(w_copies)
    for a, b in zip(RETURN_CUTS[:-1], RETURN_CUTS[1:]):
        at = pl.ds(a * SPAN, (b - a) * SPAN)
        w_copies.append(
            pltpu.make_async_copy(downw_hbm.at[0, :, at], downw_v.at[:, at], w_sem.at[len(w_copies)])
        )
    for copy in w_copies:
        copy.start()

    barrier = pltpu.get_barrier_semaphore()
    for step in range(1, n):
        pl.semaphore_signal(
            barrier, inc=1, device_id={"expert": lax.rem(me + step, n)}, device_id_type=MESH
        )
    for step in (1, ns - 1):
        pl.semaphore_signal(
            barrier, inc=1, device_id={"segment": lax.rem(seg + step, ns)}, device_id_type=MESH
        )

    gain = gain_ref[...]
    gain_lines = [
        jnp.concatenate(
            [gain[:, c * SPAN + q * LANES : c * SPAN + (q + 1) * LANES] for c in range(width // SPAN)],
            axis=1,
        )
        for q in range(QUADS)
    ]
    gain_wide = jnp.concatenate(
        [jnp.broadcast_to(line, (tokens, cols)) for line in gain_lines], axis=0
    )

    size = QUADS * group_rows
    a, b = iota((size, size), 0), iota((size, size), 1)
    unscramble = one_hot(
        ((a // RPB) % EXPERTS == b // 16)
        & (a // group_rows == (b // RPB) % QUADS)
        & (a % RPB == b % RPB)
    )
    a, b = b, a
    scramble = one_hot(
        ((a // RPB) % EXPERTS == b // 16)
        & (a // group_rows == (b // RPB) % QUADS)
        & (a % RPB == b % RPB)
    )

    def normed(values):
        squares = jnp.sum(values * values, axis=1, keepdims=True)
        total = sum(squares[q * tokens : (q + 1) * tokens] for q in range(QUADS))
        inv = lax.rsqrt(total / width + norm_eps)
        inv = jnp.concatenate([inv] * QUADS, axis=0)
        return values * inv * gain_wide

    state = [
        stack(up_ref[0].astype(jnp.float32)),
        stack(down_ref[0].astype(jnp.float32)),
    ]
    pending = []
    for tick in range(TICKS):
        pack, pick = tables([routes_ref[tick, d, 0] for d in range(DIRS)], tokens)
        rows = jnp.concatenate([normed(s) for s in state], axis=0).astype(jnp.bfloat16)
        packed = select(pack, rows).astype(jnp.bfloat16)
        send_buf[tick] = packed.reshape(EXPERTS, 16, cols)
        if tick == 0:
            pl.semaphore_wait(barrier, n + 1)

        for step in range(1, n):
            dest = lax.rem(me + step, n)
            copy = pltpu.make_async_remote_copy(
                src_ref=send_buf.at[tick, dest // shards],
                dst_ref=recv_buf.at[tick, me],
                send_sem=d_send.at[tick, step],
                recv_sem=d_recv.at[tick, me],
                device_id={"expert": dest},
                device_id_type=MESH,
            )
            copy.start()
            pending.append(copy)
        recv_buf[tick, me] = send_buf[tick, me // shards]

        for step in range(1, n):
            source = lax.rem(me + n - step, n)
            pltpu.make_async_remote_copy(
                src_ref=send_buf.at[tick, 0],
                dst_ref=recv_buf.at[tick, source],
                send_sem=d_send.at[tick, step],
                recv_sem=d_recv.at[tick, source],
                device_id={"expert": source},
                device_id_type=MESH,
            ).wait_recv()

        for g in range(n // EXPERTS):
            block = recv_buf[tick, g * EXPERTS : (g + 1) * EXPERTS].reshape(EXPERTS * 16, cols)
            straight = select(unscramble, block)
            rows_buf[g * group_rows : (g + 1) * group_rows, :] = unstack(
                straight, group_rows
            ).astype(jnp.bfloat16)

        lhs = rows_buf[...]
        for f in range(ff // tile):
            if tick == 0:
                w_copies[2 * f].wait()
                w_copies[2 * f + 1].wait()
            at = slice(f * tile, (f + 1) * tile)
            gate = jnp.dot(lhs, gate_v[:, at], preferred_element_type=jnp.float32)
            up = jnp.dot(lhs, upw_v[:, at], preferred_element_type=jnp.float32)
            hidden_buf[:, at] = (jax.nn.silu(gate) * up).astype(jnp.bfloat16)

        hidden = hidden_buf[...]
        my_place = lax.rem(me, shards) * EXPERTS + me // shards
        for r, (lo, hi) in enumerate(zip(RETURN_CUTS[:-1], RETURN_CUTS[1:])):
            if tick == 0:
                w_copies[gate_copies + r].wait()
            piece = jnp.dot(
                hidden, downw_v[:, lo * SPAN : hi * SPAN], preferred_element_type=jnp.float32
            )
            for g in range(n // EXPERTS):
                part = stack(piece[g * group_rows : (g + 1) * group_rows]).astype(jnp.bfloat16)
                block = select(scramble, part).astype(jnp.bfloat16)
                back_buf[tick, g * EXPERTS : (g + 1) * EXPERTS, :, lo * LANES : hi * LANES] = (
                    block.reshape(EXPERTS, 16, (hi - lo) * LANES)
                )
            at = pl.ds(lo * LANES, (hi - lo) * LANES)
            for step in range(1, n):
                dest = lax.rem(me + step, n)
                copy = pltpu.make_async_remote_copy(
                    src_ref=back_buf.at[tick, dest, :, at],
                    dst_ref=ret_buf.at[tick, my_place, :, at],
                    send_sem=r_send.at[tick, r, step],
                    recv_sem=r_recv.at[tick, r, my_place],
                    device_id={"expert": dest},
                    device_id_type=MESH,
                )
                copy.start()
                pending.append(copy)
            ret_buf[tick, my_place, :, lo * LANES : hi * LANES] = back_buf[
                tick, me, :, lo * LANES : hi * LANES
            ]

        weights = []
        for k in range(TOP):
            pieces = []
            for d in range(DIRS):
                pieces += [mixing_ref[tick, d, 0][:, k : k + 1]] * QUADS
            weights.append(jnp.concatenate(pieces, axis=0))
        old = jnp.concatenate(state, axis=0)
        wide = old.shape[0]
        results = []
        for r, (lo, hi) in enumerate(zip(RETURN_CUTS[:-1], RETURN_CUTS[1:])):
            at = pl.ds(lo * LANES, (hi - lo) * LANES)
            for step in range(1, n):
                source = lax.rem(me + n - step, n)
                place = lax.rem(source, shards) * EXPERTS + source // shards
                pltpu.make_async_remote_copy(
                    src_ref=back_buf.at[tick, 0, :, at],
                    dst_ref=ret_buf.at[tick, place, :, at],
                    send_sem=r_send.at[tick, r, step],
                    recv_sem=r_recv.at[tick, r, place],
                    device_id={"expert": source},
                    device_id_type=MESH,
                ).wait_recv()
            total = None
            for s in range(shards):
                block = ret_buf[
                    tick, s * EXPERTS : (s + 1) * EXPERTS, :, lo * LANES : hi * LANES
                ].reshape(EXPERTS * 16, (hi - lo) * LANES)
                found = select(pick, block)
                total = found if total is None else total + found
            mixed = total[:wide] * weights[0] + total[wide:] * weights[1]
            results.append(old[:, lo * LANES : hi * LANES] + mixed)
        result = jnp.concatenate(results, axis=1)
        half = QUADS * tokens
        halves = [result[:half], result[half:]]

        if tick + 1 < TICKS:
            state = []
            for d, (feed_ref, ahead) in enumerate(((feed_up_ref, 1), (feed_down_ref, ns - 1))):
                edge_out = ns - 1 if d == 0 else 0
                edge_in = 0 if d == 0 else ns - 1
                move_src[tick, d] = halves[d].astype(jnp.bfloat16)
                copy = pltpu.make_async_remote_copy(
                    src_ref=move_src.at[tick, d],
                    dst_ref=move_dst.at[tick, d],
                    send_sem=m_send.at[tick, d],
                    recv_sem=m_recv.at[tick, d],
                    device_id={"segment": lax.rem(seg + ahead, ns)},
                    device_id_type=MESH,
                )

                @pl.when(seg != edge_out)
                def _():
                    copy.start()

                @pl.when(seg == edge_in)
                def _():
                    move_dst[tick, d] = stack(feed_ref[tick].astype(jnp.float32)).astype(
                        jnp.bfloat16
                    )

                state.append((copy, edge_in, edge_out))
            moves = state
            state = []
            for d, (copy, edge_in, edge_out) in enumerate(moves):

                @pl.when(seg != edge_in)
                def _():
                    copy.wait_recv()

                state.append(move_dst[tick, d].astype(jnp.float32))
            for d, (copy, edge_in, edge_out) in enumerate(moves):

                @pl.when(seg != edge_out)
                def _():
                    copy.wait_send()
        else:
            out_up_ref[0] = unstack(halves[0], tokens).astype(jnp.bfloat16)
            out_down_ref[0] = unstack(halves[1], tokens).astype(jnp.bfloat16)

    for copy in pending:
        copy.wait_send()


def body(
    state_up,
    state_down,
    feed_up,
    feed_down,
    routes,
    mixing,
    norm_gain,
    gate_weight,
    up_weight,
    down_weight,
):
    n = lax.axis_size("expert")
    ns = lax.axis_size("segment")
    _, tokens, width = state_up.shape
    ff = gate_weight.shape[2]
    tile = min(GATE_TILE, ff)
    cols = width // QUADS
    parts = len(RETURN_CUTS) - 1
    bf16 = jnp.bfloat16
    vmem = pl.BlockSpec(memory_space=pltpu.VMEM)
    hbm = pl.BlockSpec(memory_space=pl.ANY)
    dma = pltpu.SemaphoreType.DMA
    return pl.pallas_call(
        functools.partial(kernel, n, ns),
        out_shape=(
            jax.ShapeDtypeStruct(state_up.shape, bf16),
            jax.ShapeDtypeStruct(state_down.shape, bf16),
        ),
        in_specs=[vmem] * 7 + [hbm] * 3,
        out_specs=(vmem, vmem),
        scratch_shapes=[
            pltpu.VMEM((width, ff), bf16),
            pltpu.VMEM((width, ff), bf16),
            pltpu.VMEM((ff, width), bf16),
            pltpu.VMEM((TICKS, EXPERTS, 16, cols), bf16),
            pltpu.VMEM((TICKS, n, 16, cols), bf16),
            pltpu.VMEM((TICKS, n, 16, cols), bf16),
            pltpu.VMEM((TICKS, n, 16, cols), bf16),
            pltpu.VMEM((n * RPB, width), bf16),
            pltpu.VMEM((n * RPB, ff), bf16),
            pltpu.VMEM((TICKS, DIRS, QUADS * tokens, cols), bf16),
            pltpu.VMEM((TICKS, DIRS, QUADS * tokens, cols), bf16),
            dma((2 * (ff // tile) + parts,)),
            dma((TICKS, n)),
            dma((TICKS, n)),
            dma((TICKS, parts, n)),
            dma((TICKS, parts, n)),
            dma((TICKS, DIRS)),
            dma((TICKS, DIRS)),
        ],
        compiler_params=pltpu.CompilerParams(collective_id=0, has_side_effects=True),
    )(
        state_up,
        state_down,
        feed_up,
        feed_down,
        routes,
        mixing,
        norm_gain,
        gate_weight,
        up_weight,
        down_weight,
    )


def solution(mesh):
    placed = (
        P("segment", "expert", None),
        P("segment", "expert", None),
        P(None, "expert", None),
        P(None, "expert", None),
        P(None, None, "segment", "expert", None),
        P(None, None, "segment", "expert", None),
        P("segment", None),
        P("segment", None, "expert"),
        P("segment", None, "expert"),
        P("segment", "expert", None),
    )
    return jax.shard_map(
        body,
        mesh=mesh,
        in_specs=placed,
        out_specs=(P("segment", "expert", None), P("segment", "expert", None)),
        check_vma=False,
    )
```

time: 128 us -> 52.2 us (0.41)
  matrix products: 48 us -> 0 us
  Pallas kernels: 0 us -> 45.5 us
  starting transfers between devices: 41.4 us -> 0 us
  waiting for transfers between devices: 16.4 us -> 0 us
  other arithmetic: 8.32 us -> 0 us
  local copies, waits for them, and re-layouts: 12 us -> 5.66 us
    dot_general x12 -> x0, matrix products: 48 us -> none  [the longest x4 28.8 us: expert_rows(): jnp.dot(hidden, down_dev, preferred_element_type=jnp.float32)]
    pallas_call x0 -> x1, Pallas kernels: none -> 45.5 us  [body(): pl.pallas_call(functools.partial(kernel, n, ns), out_shape=(jax.ShapeDtyp...]
    all_to_all x8 -> x0, starting transfers between devices: 36.7 us -> none  [the longest x2 10.2 us: body(): lax.all_to_all(expert_rows(lax.all_to_all(packed_up, 'expert', split_axis...]
    all_to_all x8 -> x0, waiting for transfers between devices: 16.4 us -> none  [the longest x2 8.57 us: body(): lax.all_to_all(expert_rows(lax.all_to_all(packed_up, 'expert', split_axis...]
    unnamed x8 -> x4, local copies, waits for them, and re-layouts: 0.02 us -> 5.66 us
    ppermute x2 -> x0, starting transfers between devices: 4.69 us -> none  [passed_along(): return lax.ppermute(block, axis, route)]
    reduce_sum x12 -> x0, other arithmetic: 4.36 us -> none  [the longest x4 2.23 us: normed(): jnp.mean(values * values, axis=-1, keepdims=True) + norm_eps]
    reshape x16 -> x0, local copies, waits for them, and re-layouts: 3.62 us -> none  [the longest x4 2.76 us: expert_rows(): return piece.reshape(sources, count, width)]
  transfers between devices with their start and end apart: 10 -> 0, of which waited for: 4 -> 0; matrix products, arithmetic and copies ran while one was open for 46% -> 0% of each run, Pallas kernels for 0% -> 0%
where the time goes in v1:
time: 52.2 us; the launch traced here: 51.8 us
  Pallas kernels  45.5 us (87%)
  local copies, waits for them, and re-layouts  5.66 us (11%)
  between operations  0.64 us (1%)
    pallas_call x1, Pallas kernels, body(): pl.pallas_call(functools.partial(kernel, n, ns), out_shape=(jax.ShapeDtyp...  45.5 us
    unnamed x4, local copies, waits for them, and re-layouts  5.66 us

profile of v1, /device:TPU:0, one launch (start us, length us, event | category | flops | bytes accessed | tf_op | source)
XLA Modules:
  0.0 51.8 jit_solution(13113940247410106930)
XLA Ops:
  0.6 1.4 %copy.12.routes_ref = s32[2,2,1,8,2]{4,3,2,1,0:T(8,128)} copy(s32[2,2,1,8,2]{3,4,2,1,0:T(2,128)} %param.14) | data formatting | bytes 512 | tf_op args[4]
  2.0 1.4 %copy.13.mixing_ref = f32[2,2,1,8,2]{4,3,2,1,0:T(8,128)} copy(f32[2,2,1,8,2]{3,4,2,1,0:T(2,128)} %param.15) | data formatting | bytes 512 | tf_op args[5]
  3.4 45.5 %shard_map.113 = (bf16[1,8,3584]{2,1,0:T(8,128)(2,1)}, bf16[1,8,3584]{2,1,0:T(8,128)(2,1)}) custom-call(bf16[1,8,3584]{2,1,0:T(8,128)(2,1)} %up_ref.1, bf16[1,8,3584]{2,1,0:T(8,128)(2,1)} %down_ref.1, bf16[1,8,3584]{2,1,0:T(8,128)(2,1)} %feed_up_ref.1, bf16[1,8,3584]{2,1,0:T(8,128)(2,1)} %feed_down_ref.1, s32[2,2,1,8,2]{4,3,2,1,0:T(8,128)} %copy.12.routes_ref, ...), custom_call_target="tpu_custom_call" | custom-call | tf_op jit(solution)/shard_map/pallas_call | solution.py:392
  48.9 1.4 %copy.16 = bf16[1,8,3584]{2,1,0:T(8,128)(2,1)} copy(bf16[1,8,3584]{2,1,0:T(8,128)(2,1)} %get-tuple-element.4) | data formatting | bytes 114688
  50.4 1.4 %copy.17 = bf16[1,8,3584]{2,1,0:T(8,128)(2,1)} copy(bf16[1,8,3584]{2,1,0:T(8,128)(2,1)} %get-tuple-element.5) | data formatting | bytes 114688

commit v2 on v0

v2 whole, which is shorter than its diff:
```python
import functools

import jax
import jax.numpy as jnp
from jax import lax
from jax.experimental import pallas as pl
from jax.experimental.pallas import tpu as pltpu
from jax.sharding import PartitionSpec as P

EXPERTS = 8
TOP = 2
TICKS = 2
CAP = 2
DIRS = 2
LANES = 128
QUADS = 4
ROWS = QUADS * CAP
SPAN = QUADS * LANES
MESH = pl.DeviceIdType.MESH

norm_eps = 1e-06

SEND_CUTS = (0, 3, 7)
RETURN_CUTS = (0, 2, 4, 7)
GATE_TILE = 256


def spans(cuts):
    return list(zip(cuts[:-1], cuts[1:]))


def iota(shape, axis):
    return lax.broadcasted_iota(jnp.int32, shape, axis)


def over(x, k):
    return x >> (k.bit_length() - 1) if k & (k - 1) == 0 else x // k


def mod(x, k):
    return x & (k - 1) if k & (k - 1) == 0 else x % k


def lane_group(rows, q):
    chunks = rows.shape[1] // SPAN
    return jnp.concatenate(
        [rows[:, c * SPAN + q * LANES : c * SPAN + (q + 1) * LANES] for c in range(chunks)], axis=1
    )


def stack(rows):
    return jnp.concatenate([lane_group(rows, q) for q in range(QUADS)], axis=0)


def interleave(groups):
    return jnp.concatenate(
        [
            group[:, c * LANES : (c + 1) * LANES]
            for c in range(groups[0].shape[1] // LANES)
            for group in groups
        ],
        axis=1,
    )


def unstack(rows, count):
    return interleave([rows[q * count : (q + 1) * count] for q in range(QUADS)])


def swap_pairs(parts):
    row = iota(parts[0].shape, 0)
    size = parts[0].shape[0]
    low = mod(row, 8) < 4
    halves = []
    for a, b in ((parts[0], parts[2]), (parts[1], parts[3])):
        halves.append(
            (
                jnp.where(low, a, pltpu.roll(b, 4, 0)),
                jnp.where(low, pltpu.roll(a, size - 4, 0), b),
            )
        )
    low = mod(row, 4) < 2
    result = []
    for side in range(2):
        a, b = halves[0][side], halves[1][side]
        result.append(jnp.where(low, a, pltpu.roll(b, 2, 0)))
        result.append(jnp.where(low, pltpu.roll(a, size - 2, 0), b))
    return result


def one_hot(condition):
    return jnp.where(condition, 1.0, 0.0).astype(jnp.bfloat16)


def select(matrix, rows):
    return jnp.dot(matrix, rows, preferred_element_type=jnp.float32)


def upright(line):
    count = line.shape[1]
    eye = iota((count, count), 0) == iota((count, count), 1)
    return jnp.sum(jnp.where(eye, line, jnp.zeros_like(line)), axis=1, keepdims=True)


def places(rows):
    tokens = rows.shape[1]
    before = iota((tokens, tokens), 1) < iota((tokens, tokens), 0)
    lying = [rows[k : k + 1, :] for k in range(TOP)]
    columns = []
    for k in range(TOP):
        col = upright(lying[k])
        same = sum(jnp.where(before & (col == line), 1, 0) for line in lying)
        place = col * CAP + jnp.sum(same, axis=1, keepdims=True)
        columns.append(jnp.concatenate([place] * QUADS, axis=0))
    return columns


def matching(shape, block_axis, tokens):
    i, j = iota(shape, block_axis), iota(shape, 1 - block_axis)
    slot = over(i, ROWS) * CAP + mod(i, CAP)
    return slot, mod(over(i, CAP), QUADS) == over(j, tokens)


def pack_matrix(columns, tokens):
    wide = QUADS * tokens
    eye = iota((wide, wide), 0) == iota((wide, wide), 1)
    slot, fits = matching((EXPERTS * ROWS, wide), 0, tokens)
    named = False
    for c in columns:
        named = named | (slot == jnp.sum(jnp.where(eye, c, 0), axis=0, keepdims=True))
    return one_hot(fits & named)


def pick_matrix(columns, tokens):
    slot, fits = matching((QUADS * tokens, EXPERTS * ROWS), 1, tokens)
    return jnp.concatenate([one_hot(fits & (slot == c)) for c in columns], axis=0)


def weight_columns(rows):
    return [jnp.concatenate([upright(rows[k : k + 1, :])] * QUADS, axis=0) for k in range(TOP)]


def kernel(
    n,
    ns,
    up_ref,
    down_ref,
    feed_up_ref,
    feed_down_ref,
    routes_ref,
    mixing_ref,
    gain_ref,
    gate_hbm,
    upw_hbm,
    downw_hbm,
    out_ref,
    gate_v,
    upw_v,
    downw_v,
    send_buf,
    recv_buf,
    back_buf,
    ret_buf,
    gate_acc,
    up_acc,
    x_in,
    routes_in,
    mixing_in,
    w_sem,
    d_send,
    d_recv,
    r_send,
    r_recv,
    m_send,
    m_recv,
):
    me = lax.axis_index("expert")
    seg = lax.axis_index("segment")
    shards = n // EXPERTS
    tokens = up_ref.shape[1]
    width = up_ref.shape[2]
    ff = gate_v.shape[1]
    tile = min(GATE_TILE, ff)
    cols = width // QUADS
    quads = n // 4
    state_refs = (up_ref, down_ref)
    feed_refs = (feed_up_ref, feed_down_ref)
    send_spans, return_spans = spans(SEND_CUTS), spans(RETURN_CUTS)

    barrier = pltpu.get_barrier_semaphore()
    for step in range(1, n):
        pl.semaphore_signal(
            barrier, inc=1, device_id={"expert": lax.rem(me + step, n)}, device_id_type=MESH
        )
    for step in (1, ns - 1):
        pl.semaphore_signal(
            barrier, inc=1, device_id={"segment": lax.rem(seg + step, ns)}, device_id_type=MESH
        )

    w_copies = []
    for lo, hi in send_spans:
        for hbm, vmem in ((gate_hbm, gate_v), (upw_hbm, upw_v)):
            at = pl.ds(lo * SPAN, (hi - lo) * SPAN)
            w_copies.append(
                pltpu.make_async_copy(hbm.at[0, at, :], vmem.at[at, :], w_sem.at[len(w_copies)])
            )
    gate_copies = len(w_copies)
    for lo, hi in return_spans:
        at = pl.ds(lo * SPAN, (hi - lo) * SPAN)
        w_copies.append(
            pltpu.make_async_copy(downw_hbm.at[0, :, at], downw_v.at[:, at], w_sem.at[len(w_copies)])
        )
    for copy in w_copies:
        copy.start()

    gain = gain_ref[...]
    gain_wide = jnp.concatenate(
        [jnp.broadcast_to(lane_group(gain, q), (tokens, cols)) for q in range(QUADS)], axis=0
    )

    def normed(values):
        squares = jnp.sum(values * values, axis=1, keepdims=True)
        total = sum(squares[q * tokens : (q + 1) * tokens] for q in range(QUADS))
        inv = lax.rsqrt(total / width + norm_eps)
        inv = jnp.concatenate([inv] * QUADS, axis=0)
        return (values * inv * gain_wide).astype(jnp.bfloat16)

    def edges(d):
        return (ns - 1, 0) if d == 0 else (0, ns - 1)

    state = [stack(ref[0].astype(jnp.float32)) for ref in state_refs]
    packs = [pack_matrix(places(routes_ref[0, d, 0]), tokens) for d in range(DIRS)]
    pending = []
    moved = []
    my_place = lax.rem(me, shards) * EXPERTS + me // shards
    for tick in range(TICKS):
        last = tick + 1 == TICKS
        for d in range(DIRS):
            packed = select(packs[d], normed(state[d]))
            for e in range(EXPERTS):
                send_buf[tick, e, d] = packed[e * ROWS : (e + 1) * ROWS].astype(jnp.bfloat16)
        if tick == 0:
            pl.semaphore_wait(barrier, n + 1)

        for g, (lo, hi) in enumerate(send_spans):
            at = pl.ds(lo * LANES, (hi - lo) * LANES)
            for step in range(1, n):
                dest = lax.rem(me + step, n)
                copy = pltpu.make_async_remote_copy(
                    src_ref=send_buf.at[tick, dest // shards, :, :, at],
                    dst_ref=recv_buf.at[tick, me, :, :, at],
                    send_sem=d_send.at[tick, g, step],
                    recv_sem=d_recv.at[tick, g, me],
                    device_id={"expert": dest},
                    device_id_type=MESH,
                )
                copy.start()
                pending.append(copy)
        recv_buf[tick, me] = send_buf[tick, me // shards]

        if not last:
            for d in range(DIRS):
                edge_out, edge_in = edges(d)
                ahead = 1 if d == 0 else ns - 1
                sources = (state_refs[d].at[0], routes_ref.at[tick, d, 0], mixing_ref.at[tick, d, 0])
                for a, (source, target) in enumerate(zip(sources, (x_in, routes_in, mixing_in))):
                    copy = pltpu.make_async_remote_copy(
                        src_ref=source,
                        dst_ref=target.at[d],
                        send_sem=m_send.at[d, a],
                        recv_sem=m_recv.at[d, a],
                        device_id={"segment": lax.rem(seg + ahead, ns)},
                        device_id_type=MESH,
                    )

                    @pl.when(seg != edge_out)
                    def _():
                        copy.start()

                    moved.append((copy, edge_out, edge_in))

                @pl.when(seg == edge_in)
                def _():
                    x_in[d] = feed_refs[d][tick]
                    routes_in[d] = routes_ref[tick, d, 0]
                    mixing_in[d] = mixing_ref[tick, d, 0]

            packs = [pack_matrix(places(routes_ref[tick + 1, d, 0]), tokens) for d in range(DIRS)]
        else:
            picks = [pick_matrix(places(routes_ref[tick, d, 0]), tokens) for d in range(DIRS)]
            weights = [weight_columns(mixing_ref[tick, d, 0]) for d in range(DIRS)]

        for g, (lo, hi) in enumerate(send_spans):
            at = pl.ds(lo * LANES, (hi - lo) * LANES)
            for step in range(1, n):
                source = lax.rem(me + n - step, n)
                pltpu.make_async_remote_copy(
                    src_ref=send_buf.at[tick, 0, :, :, at],
                    dst_ref=recv_buf.at[tick, source, :, :, at],
                    send_sem=d_send.at[tick, g, step],
                    recv_sem=d_recv.at[tick, g, source],
                    device_id={"expert": source},
                    device_id_type=MESH,
                ).wait_recv()
            parts = [
                jnp.concatenate(
                    [
                        recv_buf[tick, 4 * i + j, d, :, lo * LANES : hi * LANES].astype(jnp.float32)
                        for d in range(DIRS)
                        for i in range(quads)
                    ],
                    axis=0,
                )
                for j in range(4)
            ]
            lhs = interleave([p.astype(jnp.bfloat16) for p in swap_pairs(parts)])
            if tick == 0:
                w_copies[2 * g].wait()
                w_copies[2 * g + 1].wait()
            for f in range(ff // tile):
                at = slice(f * tile, (f + 1) * tile)
                deep = slice(lo * SPAN, hi * SPAN)
                for weight, acc in ((gate_v, gate_acc), (upw_v, up_acc)):
                    value = jnp.dot(lhs, weight[deep, at], preferred_element_type=jnp.float32)
                    if g:
                        value = acc[:, at] + value
                    acc[:, at] = value
        hidden = (jax.nn.silu(gate_acc[...]) * up_acc[...]).astype(jnp.bfloat16)

        for r, (lo, hi) in enumerate(return_spans):
            if tick == 0:
                w_copies[gate_copies + r].wait()
            piece = jnp.dot(
                hidden, downw_v[:, lo * SPAN : hi * SPAN], preferred_element_type=jnp.float32
            )
            parts = swap_pairs([lane_group(piece, q) for q in range(QUADS)])
            for j in range(4):
                for d in range(DIRS):
                    for i in range(quads):
                        row = (d * quads + i) * 8
                        back_buf[tick, 4 * i + j, d, :, lo * LANES : hi * LANES] = parts[j][
                            row : row + 8
                        ].astype(jnp.bfloat16)
            at = pl.ds(lo * LANES, (hi - lo) * LANES)
            if last:
                for step in range(1, n):
                    dest = lax.rem(me + step, n)
                    copy = pltpu.make_async_remote_copy(
                        src_ref=back_buf.at[tick, dest, :, :, at],
                        dst_ref=ret_buf.at[tick, my_place, :, :, at],
                        send_sem=r_send.at[tick, r, 0, step],
                        recv_sem=r_recv.at[tick, r, 0, my_place],
                        device_id={"expert": dest},
                        device_id_type=MESH,
                    )
                    copy.start()
                    pending.append(copy)
                ret_buf[tick, my_place, :, :, lo * LANES : hi * LANES] = back_buf[
                    tick, me, :, :, lo * LANES : hi * LANES
                ]
            else:
                for d in range(DIRS):
                    edge_out, edge_in = edges(d)
                    ahead = 1 if d == 0 else ns - 1
                    batch = []
                    for step in range(n):
                        dest = lax.rem(me + step, n)
                        copy = pltpu.make_async_remote_copy(
                            src_ref=back_buf.at[tick, dest, d, :, at],
                            dst_ref=ret_buf.at[tick, my_place, d, :, at],
                            send_sem=r_send.at[tick, r, d, step],
                            recv_sem=r_recv.at[tick, r, d, my_place],
                            device_id={"segment": lax.rem(seg + ahead, ns), "expert": dest},
                            device_id_type=MESH,
                        )
                        batch.append(copy)
                        moved.append((copy, edge_out, None))

                    @pl.when(seg != edge_out)
                    def _():
                        for copy in batch:
                            copy.start()

        if not last:
            for d in range(DIRS):

                @pl.when(seg != edges(d)[1])
                def _():
                    for copy, edge_out, edge_in in moved:
                        if edge_in == edges(d)[1]:
                            copy.wait_recv()

            picks = [pick_matrix(places(routes_in[d]), tokens) for d in range(DIRS)]
            weights = [weight_columns(mixing_in[d]) for d in range(DIRS)]
            state = [stack(x_in[d].astype(jnp.float32)) for d in range(DIRS)]

        results = [[] for _ in range(DIRS)]
        for r, (lo, hi) in enumerate(return_spans):
            at = pl.ds(lo * LANES, (hi - lo) * LANES)

            def arrived(d, step):
                source = lax.rem(me + n - step, n)
                place = lax.rem(source, shards) * EXPERTS + source // shards
                which = slice(None) if last else d
                pltpu.make_async_remote_copy(
                    src_ref=back_buf.at[tick, 0, which, :, at],
                    dst_ref=ret_buf.at[tick, place, which, :, at],
                    send_sem=r_send.at[tick, r, d, step],
                    recv_sem=r_recv.at[tick, r, d, place],
                    device_id={"expert": source},
                    device_id_type=MESH,
                ).wait_recv()

            if last:
                for step in range(1, n):
                    arrived(0, step)
            else:
                for d in range(DIRS):

                    @pl.when(seg != edges(d)[1])
                    def _():
                        for step in range(n):
                            arrived(d, step)

            for d in range(DIRS):
                total = None
                for s in range(shards):
                    block = jnp.concatenate(
                        [
                            ret_buf[tick, s * EXPERTS + e, d, :, lo * LANES : hi * LANES].astype(
                                jnp.float32
                            )
                            for e in range(EXPERTS)
                        ],
                        axis=0,
                    )
                    if not last:
                        block = jnp.where(seg == edges(d)[1], 0.0, block)
                    found = select(picks[d], block.astype(jnp.bfloat16))
                    total = found if total is None else total + found
                wide = QUADS * tokens
                mixed = total[:wide] * weights[d][0] + total[wide:] * weights[d][1]
                old = state[d][:, lo * LANES : hi * LANES]
                results[d].append(old + mixed)
        state = [jnp.concatenate(r, axis=1).astype(jnp.bfloat16) for r in results]
        if last:
            for d in range(DIRS):
                out_ref[d] = unstack(state[d].astype(jnp.float32), tokens).astype(jnp.bfloat16)
        else:
            state = [s.astype(jnp.float32) for s in state]

    for copy in pending:
        copy.wait_send()
    for d in range(DIRS):

        @pl.when(seg != edges(d)[0])
        def _():
            for copy, edge_out, _ in moved:
                if edge_out == edges(d)[0]:
                    copy.wait_send()


def body(
    state_up,
    state_down,
    feed_up,
    feed_down,
    routes,
    mixing,
    norm_gain,
    gate_weight,
    up_weight,
    down_weight,
):
    n = lax.axis_size("expert")
    ns = lax.axis_size("segment")
    _, tokens, width = state_up.shape
    ff = gate_weight.shape[2]
    cols = width // QUADS
    sends, parts = len(SEND_CUTS) - 1, len(RETURN_CUTS) - 1
    bf16 = jnp.bfloat16
    vmem = pl.BlockSpec(memory_space=pltpu.VMEM)
    hbm = pl.BlockSpec(memory_space=pl.ANY)
    dma = pltpu.SemaphoreType.DMA
    both = pl.pallas_call(
        functools.partial(kernel, n, ns),
        out_shape=jax.ShapeDtypeStruct((DIRS, tokens, width), bf16),
        in_specs=[vmem] * 7 + [hbm] * 3,
        out_specs=vmem,
        scratch_shapes=[
            pltpu.VMEM((width, ff), bf16),
            pltpu.VMEM((width, ff), bf16),
            pltpu.VMEM((ff, width), bf16),
            pltpu.VMEM((TICKS, EXPERTS, DIRS, ROWS, cols), bf16),
            pltpu.VMEM((TICKS, n, DIRS, ROWS, cols), bf16),
            pltpu.VMEM((TICKS, n, DIRS, ROWS, cols), bf16),
            pltpu.VMEM((TICKS, n, DIRS, ROWS, cols), bf16),
            pltpu.VMEM((n * DIRS * CAP, ff), jnp.float32),
            pltpu.VMEM((n * DIRS * CAP, ff), jnp.float32),
            pltpu.VMEM((DIRS, tokens, width), bf16),
            pltpu.VMEM((DIRS, TOP, tokens), jnp.int32),
            pltpu.VMEM((DIRS, TOP, tokens), jnp.float32),
            dma((2 * sends + parts,)),
            dma((TICKS, sends, n)),
            dma((TICKS, sends, n)),
            dma((TICKS, parts, DIRS, n)),
            dma((TICKS, parts, DIRS, n)),
            dma((DIRS, 3)),
            dma((DIRS, 3)),
        ],
        compiler_params=pltpu.CompilerParams(collective_id=0, has_side_effects=True),
    )(
        state_up,
        state_down,
        feed_up,
        feed_down,
        jnp.swapaxes(routes, 3, 4),
        jnp.swapaxes(mixing, 3, 4),
        norm_gain,
        gate_weight,
        up_weight,
        down_weight,
    )
    return both[0:1], both[1:2]


def solution(mesh):
    placed = (
        P("segment", "expert", None),
        P("segment", "expert", None),
        P(None, "expert", None),
        P(None, "expert", None),
        P(None, None, "segment", "expert", None),
        P(None, None, "segment", "expert", None),
        P("segment", None),
        P("segment", None, "expert"),
        P("segment", None, "expert"),
        P("segment", "expert", None),
    )
    return jax.shard_map(
        body,
        mesh=mesh,
        in_specs=placed,
        out_specs=(P("segment", "expert", None), P("segment", "expert", None)),
        check_vma=False,
    )
```

time: 128 us -> 42.9 us (0.34)
  matrix products: 48 us -> 0 us
  starting transfers between devices: 41.4 us -> 0 us
  Pallas kernels: 0 us -> 40.6 us
  waiting for transfers between devices: 16.4 us -> 0 us
  local copies, waits for them, and re-layouts: 12 us -> 1.49 us
  other arithmetic: 8.32 us -> 0 us
    dot_general x12 -> x0, matrix products: 48 us -> none  [the longest x4 28.8 us: expert_rows(): jnp.dot(hidden, down_dev, preferred_element_type=jnp.float32)]
    pallas_call x0 -> x1, Pallas kernels: none -> 40.6 us  [body(): pl.pallas_call(functools.partial(kernel, n, ns), out_shape=jax.ShapeDtype...]
    all_to_all x8 -> x0, starting transfers between devices: 36.7 us -> none  [the longest x2 10.2 us: body(): lax.all_to_all(expert_rows(lax.all_to_all(packed_up, 'expert', split_axis...]
    all_to_all x8 -> x0, waiting for transfers between devices: 16.4 us -> none  [the longest x2 8.57 us: body(): lax.all_to_all(expert_rows(lax.all_to_all(packed_up, 'expert', split_axis...]
    ppermute x2 -> x0, starting transfers between devices: 4.69 us -> none  [passed_along(): return lax.ppermute(block, axis, route)]
    reduce_sum x12 -> x0, other arithmetic: 4.36 us -> none  [the longest x4 2.23 us: normed(): jnp.mean(values * values, axis=-1, keepdims=True) + norm_eps]
    reshape x16 -> x0, local copies, waits for them, and re-layouts: 3.62 us -> none  [the longest x4 2.76 us: expert_rows(): return piece.reshape(sources, count, width)]
    another operation x4 -> x0, local copies, waits for them, and re-layouts: 2.74 us -> none  [pack_rows(): return (spread.reshape(EXPERTS * shards, CAP, width), place)]
  transfers between devices with their start and end apart: 10 -> 0, of which waited for: 4 -> 0; matrix products, arithmetic and copies ran while one was open for 46% -> 0% of each run, Pallas kernels for 0% -> 0%
where the time goes in v2:
time: 42.9 us; the launch traced here: 42.7 us
  Pallas kernels  40.6 us (95%)
  local copies, waits for them, and re-layouts  1.49 us (3%)
  between operations  0.64 us (1%)
    pallas_call x1, Pallas kernels, body(): pl.pallas_call(functools.partial(kernel, n, ns), out_shape=jax.ShapeDtype...  40.6 us
    slice x1, local copies, waits for them, and re-layouts, body(): return (both[0:1], both[1:2])  1.49 us

profile of v2, /device:TPU:0, one launch (start us, length us, event | category | flops | bytes accessed | tf_op | source)
XLA Modules:
  0.0 42.7 jit_solution(15180039975772764917)
XLA Ops:
  0.6 40.6 %shard_map.113 = bf16[2,8,3584]{2,1,0:T(8,128)(2,1)} custom-call(bf16[1,8,3584]{2,1,0:T(8,128)(2,1)} %up_ref.1, bf16[1,8,3584]{2,1,0:T(8,128)(2,1)} %down_ref.1, bf16[1,8,3584]{2,1,0:T(8,128)(2,1)} %feed_up_ref.1, bf16[1,8,3584]{2,1,0:T(8,128)(2,1)} %feed_down_ref.1, s32[2,2,1,2,8]{4,3,2,1,0:T(2,128)} %bitcast.2, f32[2,2,1,2,8]{4,3,2,1,0:T(2,128)} %bitcast.3, ...), custom_call_target="tpu_custom_call" | custom-call | tf_op jit(solution)/shard_map/pallas_call | solution.py:485
  41.2 1.5 %fusion = (bf16[1,8,3584]{2,1,0:T(8,128)(2,1)}, bf16[1,8,3584]{2,1,0:T(8,128)(2,1)}) fusion(bf16[2,8,3584]{2,1,0:T(8,128)(2,1)} %shard_map.113), kind=kLoop, calls=%fused_computation | loop fusion | bytes 229376 | tf_op jit(solution)/shard_map/slice | solution.py:524

commit v3 on v2

--- a/solution.py
+++ b/solution.py
@@ -21,7 +21,7 @@
 norm_eps = 1e-06
 
 SEND_CUTS = (0, 3, 7)
-RETURN_CUTS = (0, 2, 4, 7)
+RETURN_CUTS = (0, 3, 7)
 GATE_TILE = 256
 
 
@@ -143,13 +143,13 @@
 def kernel(
     n,
     ns,
-    up_ref,
-    down_ref,
-    feed_up_ref,
-    feed_down_ref,
-    routes_ref,
-    mixing_ref,
-    gain_ref,
+    up_hbm,
+    down_hbm,
+    feed_up_hbm,
+    feed_down_hbm,
+    routes_hbm,
+    mixing_hbm,
+    gain_hbm,
     gate_hbm,
     upw_hbm,
     downw_hbm,
@@ -166,6 +166,14 @@
     x_in,
     routes_in,
     mixing_in,
+    up_ref,
+    down_ref,
+    feed_up_ref,
+    feed_down_ref,
+    routes_ref,
+    mixing_ref,
+    gain_ref,
+    i_sem,
     w_sem,
     d_send,
     d_recv,
@@ -177,6 +185,18 @@
     me = lax.axis_index("expert")
     seg = lax.axis_index("segment")
     shards = n // EXPERTS
+    small = []
+    for source, target in (
+        (up_hbm, up_ref),
+        (down_hbm, down_ref),
+        (routes_hbm, routes_ref),
+        (gain_hbm, gain_ref),
+        (mixing_hbm, mixing_ref),
+        (feed_up_hbm, feed_up_ref),
+        (feed_down_hbm, feed_down_ref),
+    ):
+        small.append(pltpu.make_async_copy(source, target, i_sem.at[len(small)]))
+        small[-1].start()
     tokens = up_ref.shape[1]
     width = up_ref.shape[2]
     ff = gate_v.shape[1]
@@ -213,6 +233,8 @@
     for copy in w_copies:
         copy.start()
 
+    for copy in small:
+        copy.wait()
     gain = gain_ref[...]
     gain_wide = jnp.concatenate(
         [jnp.broadcast_to(lane_group(gain, q), (tokens, cols)) for q in range(QUADS)], axis=0
@@ -482,10 +504,11 @@
     vmem = pl.BlockSpec(memory_space=pltpu.VMEM)
     hbm = pl.BlockSpec(memory_space=pl.ANY)
     dma = pltpu.SemaphoreType.DMA
+    swapped = jnp.swapaxes(routes, 3, 4)
     both = pl.pallas_call(
         functools.partial(kernel, n, ns),
         out_shape=jax.ShapeDtypeStruct((DIRS, tokens, width), bf16),
-        in_specs=[vmem] * 7 + [hbm] * 3,
+        in_specs=[hbm] * 10,
         out_specs=vmem,
         scratch_shapes=[
             pltpu.VMEM((width, ff), bf16),
@@ -500,6 +523,14 @@
             pltpu.VMEM((DIRS, tokens, width), bf16),
             pltpu.VMEM((DIRS, TOP, tokens), jnp.int32),
             pltpu.VMEM((DIRS, TOP, tokens), jnp.float32),
+            pltpu.VMEM(state_up.shape, bf16),
+            pltpu.VMEM(state_down.shape, bf16),
+            pltpu.VMEM(feed_up.shape, bf16),
+            pltpu.VMEM(feed_down.shape, bf16),
+            pltpu.VMEM(swapped.shape, jnp.int32),
+            pltpu.VMEM(swapped.shape, jnp.float32),
+            pltpu.VMEM(norm_gain.shape, jnp.float32),
+            dma((7,)),
             dma((2 * sends + parts,)),
             dma((TICKS, sends, n)),
             dma((TICKS, sends, n)),
@@ -514,7 +545,7 @@
         state_down,
         feed_up,
         feed_down,
-        jnp.swapaxes(routes, 3, 4),
+        swapped,
         jnp.swapaxes(mixing, 3, 4),
         norm_gain,
         gate_weight,

time: 42.9 us -> 41.3 us (0.963)
  Pallas kernels: 40.6 us -> 39 us
    pallas_call x1, Pallas kernels: 40.6 us -> 39 us  [body(): pl.pallas_call(functools.partial(kernel, n, ns), out_shape=jax.ShapeDtype...]
where the time goes in v3:
time: 41.3 us; the launch traced here: 41.1 us
  Pallas kernels  39 us (94%)
  local copies, waits for them, and re-layouts  1.49 us (4%)
  between operations  0.64 us (2%)
    pallas_call x1, Pallas kernels, body(): pl.pallas_call(functools.partial(kernel, n, ns), out_shape=jax.ShapeDtype...  39 us
    slice x1, local copies, waits for them, and re-layouts, body(): return (both[0:1], both[1:2])  1.49 us

profile of v3, /device:TPU:0, one launch (start us, length us, event | category | flops | bytes accessed | tf_op | source)
XLA Modules:
  0.0 41.1 jit_solution(15839144812590323251)
XLA Ops:
  0.6 39.0 %shard_map.113 = bf16[2,8,3584]{2,1,0:T(8,128)(2,1)} custom-call(bf16[1,8,3584]{2,1,0:T(8,128)(2,1)} %up_hbm.1, bf16[1,8,3584]{2,1,0:T(8,128)(2,1)} %down_hbm.1, bf16[1,8,3584]{2,1,0:T(8,128)(2,1)} %feed_up_hbm.1, bf16[1,8,3584]{2,1,0:T(8,128)(2,1)} %feed_down_hbm.1, s32[2,2,1,2,8]{4,3,2,1,0:T(2,128)} %bitcast.2, f32[2,2,1,2,8]{4,3,2,1,0:T(2,128)} %bitcast.3, ...), custom_call_target="tpu_custom_call" | custom-call | tf_op jit(solution)/shard_map/pallas_call | solution.py:508
  39.6 1.5 %fusion = (bf16[1,8,3584]{2,1,0:T(8,128)(2,1)}, bf16[1,8,3584]{2,1,0:T(8,128)(2,1)}) fusion(bf16[2,8,3584]{2,1,0:T(8,128)(2,1)} %shard_map.113), kind=kLoop, calls=%fused_computation | loop fusion | bytes 229376 | tf_op jit(solution)/shard_map/slice | solution.py:555
